TPU v7x, 32 devices: a whole 2x2x4 slice. The times are simulated.
32 devices in a mesh: dp: 4 (over y, x), context: 8 (over z, core).
Axes of the slice: x: 2, y: 2, z: 4, core: 2. Of those that a mesh axis runs over, the one named last changes fastest.
Arguments:
- projected: bfloat16 [4096, 6144], P(('dp', 'context')), may hold values from -6 to 6
- short_taps: float32 [3, 6144], replicated, may hold values from -4 to 4
- long_filter: float32 [2048, 1024], P('context'), may hold values from -1.5 to 1.5
- skip_gain: float32 [2048], P('context'), may hold values from -4 to 4
- out_proj: bfloat16 [2048, 2048], P('dp'), may hold values from -0.125 to 0.125
- cotangent: bfloat16 [4096, 2048], P(('dp', 'context')), may hold values from -25 to 25
Outputs:
- grad_inputs: bfloat16 [4096, 6144], P(('dp', 'context'))
- grad_taps: float32 [3, 6144], replicated
- grad_filter: float32 [2048, 1024], P('context', 'dp')
- grad_skip: float32 [2048], P('context')
- grad_proj: float32 [2048, 2048], P(('dp', 'context'))
All inputs are finite; a program needn't handle non-finite values.
Results may differ from a plain program's by a relative error of at most 0.012.
Values may be sent and summed in bfloat16 or wider, within the bound.
No kernel may reach another device: no remote copies, remote signals or barrier semaphores. Data moves between devices by JAX's collectives and lax.ppermute only.
A program may use at most 128 MiB of HBM per device.

v0:
```python
import math
import jax
import jax.numpy as jnp
from jax import lax
from jax.sharding import PartitionSpec as P

PRECISE = lax.Precision.HIGH


def passed_along(value, axis, steps):
    count = lax.axis_size(axis)
    initial, last = (max(0, -steps), min(count, count - steps))
    return lax.ppermute(value, axis, [(source, source + steps) for source in range(initial, last)])


def angle_table(first_count, second_count, period):
    first_idx = lax.broadcasted_iota(jnp.int32, (first_count, second_count), 0)
    second_idx = lax.broadcasted_iota(jnp.int32, (first_count, second_count), 1)
    phases = first_idx * second_idx % period
    angles = phases.astype(jnp.float32) * (-2.0 * math.pi / period)
    return (jnp.cos(angles), jnp.sin(angles))


def make_tables(seq_len):
    radix_size = min(128, seq_len)
    blocks = 2 * seq_len // radix_size
    half_blocks = blocks // 2
    outer_re, outer_im = angle_table(blocks, blocks, blocks)
    twist = angle_table(blocks, radix_size, blocks * radix_size)
    inner_re, inner_im = angle_table(radix_size, radix_size, radix_size)
    first_table = jnp.concatenate([outer_re[:, :half_blocks], outer_im[:, :half_blocks]], 0)
    inner_fwd = jnp.concatenate(
        [jnp.concatenate([inner_re, inner_im], 1), jnp.concatenate([-inner_im, inner_re], 1)], 0
    )
    inner_back = jnp.concatenate(
        [jnp.concatenate([inner_re, -inner_im], 1), jnp.concatenate([inner_im, inner_re], 1)], 0
    )
    last_table = jnp.concatenate([outer_re[:half_blocks, :], outer_im[:half_blocks, :]], 1)
    return (first_table, twist, inner_fwd, inner_back, last_table)


def forward_spectrum(signal, tables):
    first_table, (twist_re, twist_im), inner_fwd, inner_back, last_table = tables
    blocks = twist_re.shape[0]
    radix_size = twist_re.shape[1]
    shaped = signal.reshape(signal.shape[0], blocks // 2, radix_size)
    first = jnp.einsum("kn,cnm->ckm", first_table, shaped, precision=PRECISE)
    first_re = first[:, :blocks]
    first_im = first[:, blocks:]
    turned = jnp.concatenate(
        [first_re * twist_re - first_im * twist_im, first_re * twist_im + first_im * twist_re], 2
    )
    return jnp.einsum("ckn,nm->ckm", turned, inner_fwd, precision=PRECISE)


def spectral_product(left, right, conjugate_left):
    width = left.shape[2] // 2
    left_re, left_im = (left[:, :, :width], left[:, :, width:])
    right_re, right_im = (right[:, :, :width], right[:, :, width:])
    if conjugate_left:
        return jnp.concatenate(
            [left_re * right_re + left_im * right_im, left_re * right_im - left_im * right_re], 2
        )
    return jnp.concatenate(
        [left_re * right_re - left_im * right_im, left_re * right_im + left_im * right_re], 2
    )


def inverse_real(spectrum, tables):
    first_table, (twist_re, twist_im), inner_fwd, inner_back, last_table = tables
    blocks = twist_re.shape[0]
    radix_size = twist_re.shape[1]
    undo = jnp.einsum("ckn,nm->ckm", spectrum, inner_back, precision=PRECISE)
    undo_re = undo[:, :, :radix_size]
    undo_im = undo[:, :, radix_size:]
    back = jnp.concatenate(
        [undo_re * twist_re + undo_im * twist_im, undo_im * twist_re - undo_re * twist_im], 1
    )
    result = jnp.einsum("nk,ckm->cnm", last_table, back, precision=PRECISE)
    return result.reshape(spectrum.shape[0], blocks // 2 * radix_size) / (blocks * radix_size)


def body(projected, short_taps, long_filter, skip_gain, out_proj, cotangent):
    tok_rows = projected.shape[0]
    chan_all = projected.shape[1] // 3
    prev_rows = passed_along(projected[tok_rows - 2 :], "context", 1)
    extended = jnp.concatenate([prev_rows, projected], 0).astype(jnp.float32)
    current = extended[2:]
    once_back = extended[1 : tok_rows + 1]
    twice_back = extended[:tok_rows]
    mixed = short_taps[0] * current + short_taps[1] * once_back + short_taps[2] * twice_back
    query = mixed[:, :chan_all].astype(jnp.bfloat16)
    keyed = mixed[:, chan_all : 2 * chan_all].astype(jnp.bfloat16)
    valued = mixed[:, 2 * chan_all :].astype(jnp.bfloat16)
    product = (keyed.astype(jnp.float32) * valued.astype(jnp.float32)).astype(jnp.bfloat16)
    product_chan = lax.all_to_all(product.T, "context", split_axis=0, concat_axis=1, tiled=True)
    seq_len = product_chan.shape[1]
    tables = make_tables(seq_len)
    prod_f = product_chan.astype(jnp.float32)
    filter_spec = forward_spectrum(long_filter, tables)
    prod_spec = forward_spectrum(prod_f, tables)
    long_chan = (
        inverse_real(spectral_product(filter_spec, prod_spec, False), tables)
        + skip_gain[:, None] * prod_f
    )
    long_tok = lax.all_to_all(
        long_chan.astype(jnp.bfloat16), "context", split_axis=1, concat_axis=0, tiled=True
    ).T
    gate = (query.astype(jnp.float32) * long_tok.astype(jnp.float32)).astype(jnp.bfloat16)
    grad_gate = lax.dot_general(
        cotangent,
        lax.all_gather(out_proj, "dp", axis=0, tiled=True),
        (((1,), (1,)), ((), ())),
        preferred_element_type=jnp.float32,
    ).astype(jnp.bfloat16)
    grad_rows = lax.psum_scatter(
        lax.dot_general(
            gate, cotangent, (((0,), (0,)), ((), ())), preferred_element_type=jnp.float32
        ),
        ("dp", "context"),
        scatter_dimension=0,
        tiled=True,
    )
    grad_query = grad_gate.astype(jnp.float32) * long_tok.astype(jnp.float32)
    grad_long = (grad_gate.astype(jnp.float32) * query.astype(jnp.float32)).astype(jnp.bfloat16)
    grad_chan = lax.all_to_all(
        grad_long.T, "context", split_axis=0, concat_axis=1, tiled=True
    ).astype(jnp.float32)
    grad_spec = forward_spectrum(grad_chan, tables)
    back_chan = (
        inverse_real(spectral_product(filter_spec, grad_spec, True), tables)
        + skip_gain[:, None] * grad_chan
    )
    filter_local = inverse_real(spectral_product(prod_spec, grad_spec, True), tables)
    grad_product = lax.all_to_all(
        back_chan.astype(jnp.bfloat16), "context", split_axis=1, concat_axis=0, tiled=True
    ).T
    scale_factor = 1.0 / math.sqrt(seq_len * lax.axis_size("dp"))
    grad_filter = (
        lax.psum_scatter(filter_local, "dp", scatter_dimension=1, tiled=True) * scale_factor
    )
    grad_skip = lax.psum(jnp.sum(grad_chan * prod_f, axis=1), "dp") * scale_factor
    grad_key = grad_product.astype(jnp.float32) * valued.astype(jnp.float32)
    grad_value = grad_product.astype(jnp.float32) * keyed.astype(jnp.float32)
    grad_mixed = jnp.concatenate([grad_query, grad_key, grad_value], 1)
    next_rows = passed_along(grad_mixed[:2].astype(jnp.bfloat16), "context", -1).astype(jnp.float32)
    grad_ext = jnp.concatenate([grad_mixed, next_rows], 0)
    grad_inputs = (
        short_taps[0] * grad_ext[:tok_rows]
        + short_taps[1] * grad_ext[1 : tok_rows + 1]
        + short_taps[2] * grad_ext[2:]
    ).astype(jnp.bfloat16)
    taps_terms = jnp.stack(
        [
            jnp.sum(grad_mixed * current, 0),
            jnp.sum(grad_mixed * once_back, 0),
            jnp.sum(grad_mixed * twice_back, 0),
        ]
    )
    grad_taps = lax.psum(taps_terms, ("dp", "context")) * scale_factor
    return (grad_inputs, grad_taps, grad_filter, grad_skip, grad_rows * scale_factor)


def solution(mesh):
    placed = (
        P(("dp", "context"), None),
        P(),
        P("context", None),
        P("context"),
        P("dp", None),
        P(("dp", "context"), None),
    )
    return jax.shard_map(
        body,
        mesh=mesh,
        in_specs=placed,
        out_specs=(
            P(("dp", "context"), None),
            P(),
            P("context", "dp"),
            P("context"),
            P(("dp", "context"), None),
        ),
        check_vma=False,
    )
```

profile of v0, /device:TPU:0, one launch (start us, length us, event | category | flops | bytes accessed | tf_op | source)
XLA Modules:
  0.0 625.5 jit_solution(3541810269681701199)
XLA Ops:
  15.6 84.6 %all-gather.2.cloned.1.call-done = bf16[2048,2048]{1,0:T(8,128)(2,1)} async-done(((bf16[512,2048]{1,0:T(8,128)(2,1)}), bf16[2048,2048]{1,0:T(8,128)(2,1)}) %all-gather.2.cloned.1.call-update) | async-done | bytes 8388624 | tf_op jit(solution)/shard_map/all_gather | solution.py:112
  100.2 6.2 fusion.21
  108.6 4.6 all-to-all-start.2
  115.5 3.9 convolution_bitcast_fusion.2
  119.5 9.1 %all-to-all-done.2 = bf16[8,256,128]{2,1,0:T(8,128)(2,1)S(1)} async-done(((bf16[8,256,128]{2,1,0:T(8,128)(2,1)}), bf16[8,256,128]{2,1,0:T(8,128)(2,1)S(1)}, u32[]{:S(2)}, u32[]{:S(2)}) %all-to-all-start.2) | async-done | bytes 524320 | tf_op jit(solution)/shard_map/all_to_all | solution.py:126
  132.6 4.2 fusion.16
  136.8 4.2 fusion.12
  145.5 5.5 copy.61
  151.0 4.0 fusion.68
  159.0 17.8 %all_to_all.52 = bf16[256,8,128]{2,0,1:T(8,128)(2,1)S(1)} all-to-all(bf16[256,8,128]{2,0,1:T(8,128)(2,1)S(1)} %copy.52), channel_id=1, replica_groups=mesh['dp'=4,'context'=8] {'context'}, dimensions={1} | all-to-all | bytes 1048576 | tf_op jit(solution)/shard_map/all_to_all | solution.py:135
  181.2 17.8 %all_to_all.53 = bf16[8,256,128]{2,1,0:T(8,128)(2,1)S(1)} all-to-all(bf16[8,256,128]{2,1,0:T(8,128)(2,1)S(1)} %bitcast.96), channel_id=1, replica_groups=mesh['dp'=4,'context'=8] {'context'}, dimensions={0} | all-to-all | bytes 1048576 | tf_op jit(solution)/shard_map/all_to_all | solution.py:96
  202.0 4.1 fusion.14
  206.1 4.4 multiply_add_fusion.1
  210.5 4.6 pad_maximum_fusion.5
  215.1 5.5 copy.64
  220.6 6.1 fusion.66
  229.0 5.6 copy.58
  234.7 4.3 fusion.70
  245.1 17.8 %all_to_all.54 = bf16[256,8,128]{2,0,1:T(8,128)(2,1)S(1)} all-to-all(bf16[256,8,128]{2,0,1:T(8,128)(2,1)S(1)} %copy.43), channel_id=1, replica_groups=mesh['dp'=4,'context'=8] {'context'}, dimensions={1} | all-to-all | bytes 1048576 | tf_op jit(solution)/shard_map/all_to_all | solution.py:106
  282.0 9.1 %fusion.53 = f32[2048,2048]{1,0:T(8,128)} fusion(bf16[128,2048]{1,0:T(8,128)(2,1)S(1)} %copy-done, f32[2048,128]{0,1:T(8,128)S(1)} %copy-done.10, bf16[128,6144]{1,0:T(8,128)(2,1)} %copy-done.12), kind=kOutput, calls=%fused_computation.82 | convolution fusion | flops 1074528256 | bytes 18874368 | tf_op jit(solution)/shard_map/dot_general | solution.py:117
  293.5 8.9 %psum.15 = f32[256]{0:T(256)S(1)} all-reduce(f32[256]{0:T(256)S(1)} %fusion.52), channel_id=1, replica_groups=mesh['dp'=4,'context'=8] {'dp'}, use_global_device_ids=true, to_apply=%region_6.7 | all-reduce | flops 256 | bytes 2048 | tf_op jit(solution)/shard_map/psum | solution.py:142
  303.0 93.5 %all-reduce.2.cloned.1.call-done = f32[3,6144]{1,0:T(4,128)} async-done(((f32[3,6144]{1,0:T(4,128)}), f32[3,6144]{1,0:T(4,128)}) %all-reduce.2.cloned.1.call-update) | async-done | bytes 73744 | tf_op jit(solution)/shard_map/psum | solution.py:160
  398.0 29.9 %reduce-scatter.3.cloned.1.call-done = f32[256,256]{1,0:T(8,128)} async-done(((f32[256,1024]{1,0:T(8,128)}), f32[256,256]{1,0:T(8,128)}) %reduce-scatter.3.cloned.1.call-update) | async-done | bytes 262160 | tf_op jit(solution)/shard_map/reduce_scatter | solution.py:140
  429.6 187.3 %reduce-scatter.5.cloned.1.call-done = f32[64,2048]{1,0:T(8,128)} async-done(((f32[2048,2048]{1,0:T(8,128)}), f32[64,2048]{1,0:T(8,128)}) %reduce-scatter.5.cloned.1.call-update) | async-done | bytes 524304 | tf_op jit(solution)/shard_map/reduce_scatter | solution.py:116
  (108 shorter events, 67.9 us)
Async XLA Ops:
  7.2 93.1 %copy-start = (bf16[128,2048]{1,0:T(8,128)(2,1)S(1)}, bf16[128,2048]{1,0:T(8,128)(2,1)}, u32[]{:S(2)}) copy-start(bf16[128,2048]{1,0:T(8,128)(2,1)} %param.11) | copy-start | bytes 1572868
  7.2 5.3 copy-start.20
  7.2 93.0 %all-gather.2.cloned.1.call-start = ((), (), s32[]{:S(2)}) async-start(), calls=%async_computation.6 | async-start | bytes 10485760 | tf_op jit(solution)/shard_map/all_gather | solution.py:112
  8.8 3.6 collective-permute-start
  12.9 1.7 copy-start.1
  15.6 90.9 %copy-start.12 = (bf16[128,6144]{1,0:T(8,128)(2,1)}, bf16[128,6144]{1,0:T(8,128)(2,1)S(1)}, u32[]{:S(2)}) copy-start(bf16[128,6144]{1,0:T(8,128)(2,1)S(1)} %add_convert_fusion) | copy-start | bytes 4718596
  108.6 20.0 %all-to-all-start.2 = ((bf16[8,256,128]{2,1,0:T(8,128)(2,1)}), bf16[8,256,128]{2,1,0:T(8,128)(2,1)S(1)}, u32[]{:S(2)}, u32[]{:S(2)}) async-start(bf16[8,256,128]{2,1,0:T(8,128)(2,1)} %bitcast.17), calls=%async_computation.2 | async-start | bytes 1048576 | tf_op jit(solution)/shard_map/all_to_all | solution.py:126
  113.2 283.3 %all-reduce.2.cloned.1.call-start = ((), (), s32[]{:S(2)}) async-start(), calls=%async_computation.7 | async-start | bytes 196608 | tf_op jit(solution)/shard_map/psum | solution.py:160
  128.6 26.9 %copy-start.13 = (bf16[8,256,128]{2,1,0:T(8,128)(2,1)}, bf16[8,256,128]{2,1,0:T(8,128)(2,1)S(1)}, u32[]{:S(2)}) copy-start(bf16[8,256,128]{2,1,0:T(8,128)(2,1)S(1)} %all-to-all-done.2) | copy-start | bytes 1572868
  128.6 2.4 copy-start.7
  136.8 4.2 copy-start.3
  141.0 1.9 copy-start.5
  201.9 4.1 copy-start.4
  202.0 4.1 copy-start.6
  220.6 6.1 copy-start.18
  220.6 6.1 copy-start.19
  234.7 4.3 copy-start.8
  239.0 2.8 copy-start.16
  262.9 5.3 copy-start.9
  268.4 3.1 collective-permute-start.1
  271.5 1.9 copy-start.2
  277.2 150.8 %reduce-scatter.3.cloned.1.call-start = ((), (), s32[]{:S(2)}) async-start(), calls=%async_computation.8 | async-start | bytes 1310720 | tf_op jit(solution)/shard_map/reduce_scatter | solution.py:140
  277.3 4.8 copy-start.10
  282.0 334.9 %reduce-scatter.5.cloned.1.call-start = ((), (), s32[]{:S(2)}) async-start(), calls=%async_computation.9 | async-start | bytes 17301504 | tf_op jit(solution)/shard_map/reduce_scatter | solution.py:116
  (5 other events, 4.7 us)
Sparse Core Ops, SparseCore 0:
  9.9 90.2 all-gather.1
  277.3 119.1 all-reduce.1
  399.4 28.5 reduce-scatter.2
  430.2 186.6 reduce-scatter.4
where the time goes:
time: 631 us; the launch traced here: 626 us
  waiting for transfers between devices  407 us (65%)
  blocking collectives  62.2 us (10%)
  matrix products  58.9 us (9%)
  other arithmetic  39.3 us (6%)
  local copies, waits for them, and re-layouts  35.3 us (6%)
  between operations  14.5 us (2%)
  starting transfers between devices  8.42 us (1%)
    reduce_scatter x1, waiting for transfers between devices, body(): lax.psum_scatter(lax.dot_general(gate, cotangent, (((0,), (0,)), ((), ())...  187 us
    psum x1, waiting for transfers between devices, body(): grad_taps = lax.psum(taps_terms, ('dp', 'context')) * scale_factor  93.5 us
    all_gather x1, waiting for transfers between devices, body(): lax.all_gather(out_proj, 'dp', axis=0, tiled=True)  84.6 us
    reduce_scatter x1, waiting for transfers between devices, body(): lax.psum_scatter(filter_local, 'dp', scatter_dimension=1, tiled=True)  29.9 us
    all_to_all x1, blocking collectives, body(): lax.all_to_all(back_chan.astype(jnp.bfloat16), 'context', split_axis=1, c...  17.8 us
    all_to_all x1, blocking collectives, body(): lax.all_to_all(product.T, 'context', split_axis=0, concat_axis=1, tiled=T...  17.8 us
    all_to_all x1, blocking collectives, body(): lax.all_to_all(long_chan.astype(jnp.bfloat16), 'context', split_axis=1, c...  17.8 us
    dot_general x3, matrix products, inverse_real(): undo = jnp.einsum('ckn,nm->ckm', spectrum, inner_back, precision=PRECISE)  14.4 us
  transfers between devices with their start and end apart: 7, of which 6 were waited for; matrix products, arithmetic and copies ran while one was open for 5% of the time, Pallas kernels for 0%

commit v1 on v0

--- a/solution.py
+++ b/solution.py
@@ -5,6 +5,28 @@
 from jax.sharding import PartitionSpec as P
 
 PRECISE = lax.Precision.HIGH
+
+
+def laid_out(blocks, dim):
+    lengths = list(blocks.shape[1:])
+    lengths[dim] *= blocks.shape[0]
+    return jnp.moveaxis(blocks, 0, dim).reshape(lengths)
+
+
+def ring_gather(value, axis, dim):
+    size = lax.axis_size(axis)
+    pairs = [(i, (i + 1) % size) for i in range(size)]
+    back = [(b, a) for a, b in pairs]
+    lower, upper = ([], [])
+    for turn in range(size - 1):
+        if turn % 2 == 0:
+            lower.append(lax.ppermute(lower[-1] if lower else value, axis, pairs))
+        else:
+            upper.append(lax.ppermute(upper[-1] if upper else value, axis, back))
+    blocks = jnp.stack([*lower[::-1], value, *upper])
+    shift = lax.axis_index(axis) - len(lower)
+    blocks = blocks[(jnp.arange(size) - shift) % size]
+    return laid_out(blocks, dim)
 
 
 def passed_along(value, axis, steps):
@@ -109,7 +131,7 @@
     gate = (query.astype(jnp.float32) * long_tok.astype(jnp.float32)).astype(jnp.bfloat16)
     grad_gate = lax.dot_general(
         cotangent,
-        lax.all_gather(out_proj, "dp", axis=0, tiled=True),
+        ring_gather(out_proj, "dp", 0),
         (((1,), (1,)), ((), ())),
         preferred_element_type=jnp.float32,
     ).astype(jnp.bfloat16)

time: 631 us -> 604 us (0.957)
  waiting for transfers between devices: 407 us -> 346 us
  blocking collectives: 62.2 us -> 27.9 us
  other arithmetic: 39.3 us -> 71.6 us
  local copies, waits for them, and re-layouts: 35.3 us -> 50.5 us
  starting transfers between devices: 8.42 us -> 21.1 us
    reduce_scatter x1, waiting for transfers between devices: 187 us -> 60 us  [body(): lax.psum_scatter(lax.dot_general(gate, cotangent, (((0,), (0,)), ((), ())...]
    ppermute x0 -> x3, waiting for transfers between devices: none -> 120 us  [the longest x2 83.1 us: ring_gather(): lower.append(lax.ppermute(lower[-1] if lower else value, axis, pairs))]
    all_gather x1 -> x0, waiting for transfers between devices: 84.6 us -> none  [body(): lax.all_gather(out_proj, 'dp', axis=0, tiled=True)]
    psum x1, waiting for transfers between devices: 93.5 us -> 132 us  [body(): grad_taps = lax.psum(taps_terms, ('dp', 'context')) * scale_factor]
    all_to_all x2 -> x0, blocking collectives: 35.5 us -> none  [the longest x1 17.8 us: body(): lax.all_to_all(back_chan.astype(jnp.bfloat16), 'context', split_axis=1, c...]
    reduce_scatter x1, waiting for transfers between devices: 29.9 us -> 0.01 us  [body(): lax.psum_scatter(filter_local, 'dp', scatter_dimension=1, tiled=True)]
    all_to_all x0 -> x2, waiting for transfers between devices: none -> 24.1 us  [the longest x1 13.3 us: body(): lax.all_to_all(product.T, 'context', split_axis=0, concat_axis=1, tiled=T...]
    gather x0 -> x3, local copies, waits for them, and re-layouts: none -> 13.7 us  [ring_gather(): blocks = blocks[(jnp.arange(size) - shift) % size]]
  transfers between devices with their start and end apart: 7 -> 11, of which waited for: 6 -> 9; matrix products, arithmetic and copies ran while one was open for 5% -> 8% of each run, Pallas kernels for 0% -> 0%
where the time goes in v1:
time: 604 us; the launch traced here: 596 us
  waiting for transfers between devices  346 us (57%)
  other arithmetic  71.6 us (12%)
  matrix products  63.1 us (10%)
  local copies, waits for them, and re-layouts  50.5 us (8%)
  blocking collectives  27.9 us (5%)
  starting transfers between devices  21.1 us (3%)
  between operations  16.1 us (3%)
    psum x1, waiting for transfers between devices, body(): grad_taps = lax.psum(taps_terms, ('dp', 'context')) * scale_factor  132 us
    ppermute x2, waiting for transfers between devices, ring_gather(): lower.append(lax.ppermute(lower[-1] if lower else value, axis, pairs))  83.1 us
    reduce_scatter x1, waiting for transfers between devices, body(): lax.psum_scatter(lax.dot_general(gate, cotangent, (((0,), (0,)), ((), ())...  60 us
    ppermute x1, waiting for transfers between devices, ring_gather(): upper.append(lax.ppermute(upper[-1] if upper else value, axis, back))  37 us
    all_to_all x1, blocking collectives, body(): lax.all_to_all(long_chan.astype(jnp.bfloat16), 'context', split_axis=1, c...  18.9 us
    dot_general x3, matrix products, inverse_real(): undo = jnp.einsum('ckn,nm->ckm', spectrum, inner_back, precision=PRECISE)  16.6 us
    gather x3, local copies, waits for them, and re-layouts, ring_gather(): blocks = blocks[(jnp.arange(size) - shift) % size]  13.7 us
    all_to_all x1, waiting for transfers between devices, body(): lax.all_to_all(product.T, 'context', split_axis=0, concat_axis=1, tiled=T...  13.3 us
  transfers between devices with their start and end apart: 11, of which 9 were waited for; matrix products, arithmetic and copies ran while one was open for 8% of the time, Pallas kernels for 0%

profile of v1, /device:TPU:0, one launch (start us, length us, event | category | flops | bytes accessed | tf_op | source)
XLA Modules:
  0.0 596.4 jit_solution(4377127938033035848)
XLA Ops:
  19.1 39.6 %collective-permute-done = bf16[512,2048]{1,0:T(8,128)(2,1)} collective-permute-done((bf16[512,2048]{1,0:T(8,128)(2,1)}, bf16[512,2048]{1,0:T(8,128)(2,1)}, u32[]{:S(2)}, u32[]{:S(2)}) %collective-permute-start) | collective-permute-done | bytes 2097184 | tf_op jit(solution)/shard_map/ppermute | solution.py:23
  62.4 4.8 add_convert_fusion
  67.2 37.0 %collective-permute-done.2 = bf16[512,2048]{1,0:T(8,128)(2,1)} collective-permute-done((bf16[512,2048]{1,0:T(8,128)(2,1)}, bf16[512,2048]{1,0:T(8,128)(2,1)}, u32[]{:S(2)}, u32[]{:S(2)}) %collective-permute-start.2) | collective-permute-done | bytes 2097184 | tf_op jit(solution)/shard_map/ppermute | solution.py:25
  104.2 43.4 %collective-permute-done.1 = bf16[512,2048]{1,0:T(8,128)(2,1)S(1)} collective-permute-done((bf16[512,2048]{1,0:T(8,128)(2,1)}, bf16[512,2048]{1,0:T(8,128)(2,1)S(1)}, u32[]{:S(2)}, u32[]{:S(2)}) %collective-permute-start.1) | collective-permute-done | bytes 2097184 | tf_op jit(solution)/shard_map/ppermute | solution.py:23
  154.8 5.0 gather_fusion.1
  159.8 5.0 gather_fusion
  164.8 8.2 %pad_maximum_fusion.1 = bf16[4,512,2048]{2,1,0:T(8,128)(2,1)} fusion(bf16[4,512,1024]{2,1,0:T(8,128)(2,1)} %gather_fusion.1, bf16[4,512,1024]{2,1,0:T(8,128)(2,1)} %gather_fusion), kind=kLoop, calls=%fused_computation.3 | loop fusion | flops 16777216 | bytes 16777216
  173.0 7.1 %fusion.50 = (bf16[128,2048]{0,1:T(8,128)(2,1)}, bf16[128,2048]{0,1:T(8,128)(2,1)}, f32[128,2048]{0,1:T(8,128)}) fusion(bf16[128,6144]{0,1:T(8,128)(2,1)S(1)} %add_convert_fusion, bf16[2048,2048]{1,0:T(8,128)(2,1)} %bitcast.105, bf16[128,2048]{1,0:T(8,128)(2,1)S(1)} %copy-done), kind=kOutput, calls=%fused_computation.82 | convolution fusion | flops 1076101120 | bytes 12582912 | tf_op jit(solution)/shard_map/dot_general | solution.py:132
  180.0 5.1 all-to-all-start
  187.2 13.3 %all-to-all-done = bf16[8,256,128]{2,1,0:T(8,128)(2,1)S(1)} async-done(((bf16[8,256,128]{2,1,0:T(8,128)(2,1)}), bf16[8,256,128]{2,1,0:T(8,128)(2,1)S(1)}, u32[]{:S(2)}, u32[]{:S(2)}) %all-to-all-start) | async-done | bytes 524320 | tf_op jit(solution)/shard_map/all_to_all | solution.py:118
  211.4 8.0 %all-to-all-done.2 = bf16[8,256,128]{2,1,0:T(8,128)(2,1)S(1)} async-done(((bf16[8,256,128]{2,1,0:T(8,128)(2,1)}), bf16[8,256,128]{2,1,0:T(8,128)(2,1)S(1)}, u32[]{:S(2)}, u32[]{:S(2)}) %all-to-all-start.2) | async-done | bytes 524320 | tf_op jit(solution)/shard_map/all_to_all | solution.py:148
  248.3 4.6 pad_maximum_fusion.8
  252.8 5.5 copy.68
  258.4 6.1 %fusion.62 = f32[256,16,256]{2,1,0:T(8,128)} fusion(f32[256,16,256]{2,1,0:T(8,128)} %copy.68, f32[128,128]{0,1:T(8,128)S(1)} %get-tuple-element.61, f32[128,128]{0,1:T(8,128)S(1)} %get-tuple-element.60, f32[128,128]{0,1:T(8,128)S(1)} %fusion.79), kind=kOutput, calls=%fused_computation.101 | convolution fusion | flops 1610809344 | bytes 8585216 | tf_op jit(solution)/shard_map/ckn,nm->ckm/dot_general | solution.py:95
  266.8 5.5 copy.62
  272.4 6.2 %fusion.66 = f32[256,16,256]{2,1,0:T(8,128)} fusion(f32[256,16,256]{2,1,0:T(8,128)} %copy.62, f32[128,128]{0,1:T(8,128)S(1)} %get-tuple-element.61, f32[128,128]{0,1:T(8,128)S(1)} %get-tuple-element.60, f32[128,128]{0,1:T(8,128)S(1)} %fusion.79), kind=kOutput, calls=%fused_computation.103 | convolution fusion | flops 1610809344 | bytes 8585216 | tf_op jit(solution)/shard_map/ckn,nm->ckm/dot_general | solution.py:95
  280.8 5.5 copy.65
  308.2 10.8 %all-to-all-done.3 = bf16[256,8,128]{2,0,1:T(8,128)(2,1)} async-done(((bf16[256,8,128]{2,0,1:T(8,128)(2,1)}), bf16[256,8,128]{2,0,1:T(8,128)(2,1)}, u32[]{:S(2)}, u32[]{:S(2)}) %all-to-all-start.3) | async-done | bytes 524320 | tf_op jit(solution)/shard_map/all_to_all | solution.py:157
  318.9 18.9 %all_to_all.52 = bf16[256,8,128]{2,0,1:T(8,128)(2,1)S(1)} all-to-all(bf16[256,8,128]{2,0,1:T(8,128)(2,1)} %copy.47), channel_id=1, replica_groups=mesh['dp'=4,'context'=8] {'context'}, dimensions={1} | all-to-all | bytes 1048576 | tf_op jit(solution)/shard_map/all_to_all | solution.py:128
  354.0 10.3 %multiply_reduce_fusion.2 = (f32[6144]{0:T(1024)S(1)}, f32[6144]{0:T(1024)S(1)}, f32[6144]{0:T(1024)S(1)}, bf16[128,6144]{0,1:T(8,128)(2,1)}) fusion(f32[130,6144]{0,1:T(8,128)S(1)} %bitcast.104, f32[128,2048]{0,1:T(8,128)S(1)} %copy-done.5, f32[128,2048]{0,1:T(8,128)S(1)} %copy-done.3, f32[128,2048]{0,1:T(8,128)S(1)} %copy-done.7, ...), kind=kLoop, calls=%fused_computation.39 | loop fusion | flops 10991616 | bytes 20594688 | tf_op jit(solution)/shard_map/reduce_sum | solution.py:177
  370.1 8.1 %fusion.109 = f32[2048,2048]{1,0:T(8,128)} fusion(bf16[128,2048]{0,1:T(8,128)(2,1)S(1)} %copy-done.20, bf16[128,2048]{1,0:T(8,128)(2,1)S(1)} %copy-done), kind=kOutput, calls=%fused_computation.162 | convolution fusion | flops 1073741824 | bytes 17825792 | tf_op jit(solution)/shard_map/dot_general | solution.py:139
  380.3 9.0 %psum.15 = f32[256]{0:T(256)S(1)} all-reduce(f32[256]{0:T(256)S(1)} %fusion.53), channel_id=1, replica_groups=mesh['dp'=4,'context'=8] {'dp'}, use_global_device_ids=true, to_apply=%region_6.7 | all-reduce | flops 256 | bytes 2048 | tf_op jit(solution)/shard_map/psum | solution.py:164
  391.5 132.1 %all-reduce.2.cloned.1.call-done = f32[3,6144]{1,0:T(4,128)} async-done(((f32[3,6144]{1,0:T(4,128)}), f32[3,6144]{1,0:T(4,128)}) %all-reduce.2.cloned.1.call-update) | async-done | bytes 73744 | tf_op jit(solution)/shard_map/psum | solution.py:182
  526.8 60.0 %reduce-scatter.5.cloned.1.call-done = f32[64,2048]{1,0:T(8,128)} async-done(((f32[2048,2048]{1,0:T(8,128)}), f32[64,2048]{1,0:T(8,128)}) %reduce-scatter.5.cloned.1.call-update) | async-done | bytes 524304 | tf_op jit(solution)/shard_map/reduce_scatter | solution.py:138
  (123 shorter events, 121.1 us)
Async XLA Ops:
  8.0 165.0 %copy-start = (bf16[128,2048]{1,0:T(8,128)(2,1)S(1)}, bf16[128,2048]{1,0:T(8,128)(2,1)}, u32[]{:S(2)}) copy-start(bf16[128,2048]{1,0:T(8,128)(2,1)} %param.11) | copy-start | bytes 1572868
  8.0 50.7 %collective-permute-start = (bf16[512,2048]{1,0:T(8,128)(2,1)}, bf16[512,2048]{1,0:T(8,128)(2,1)}, u32[]{:S(2)}, u32[]{:S(2)}) collective-permute-start(bf16[512,2048]{1,0:T(8,128)(2,1)} %param.10), channel_id=1, source_target_pairs={{0,8},{8,16},{16,24},{24,0},{1,9},{9,17},{17,25},{25,1},{2,10},{10... | collective-permute-start | bytes 6291464 | tf_op jit(solution)/shard_map/ppermute | solution.py:23
  11.0 93.2 %collective-permute-start.2 = (bf16[512,2048]{1,0:T(8,128)(2,1)}, bf16[512,2048]{1,0:T(8,128)(2,1)}, u32[]{:S(2)}, u32[]{:S(2)}) collective-permute-start(bf16[512,2048]{1,0:T(8,128)(2,1)} %param.10), channel_id=1, source_target_pairs={{8,0},{16,8},{24,16},{0,24},{9,1},{17,9},{25,17},{1,25},{10,2},{18... | collective-permute-start | bytes 6291464 | tf_op jit(solution)/shard_map/ppermute | solution.py:25
  13.0 4.5 collective-permute-start.3
  58.7 88.9 %collective-permute-start.1 = (bf16[512,2048]{1,0:T(8,128)(2,1)}, bf16[512,2048]{1,0:T(8,128)(2,1)S(1)}, u32[]{:S(2)}, u32[]{:S(2)}) collective-permute-start(bf16[512,2048]{1,0:T(8,128)(2,1)} %collective-permute-done), channel_id=1, source_target_pairs={{0,8},{8,16},{16,24},{24,0},{1,9},{9,17},{17,25},{25,1},{2,10},{10... | collective-permute-start | bytes 6291464 | tf_op jit(solution)/shard_map/ppermute | solution.py:23
  62.4 85.3 %copy-start.21 = (bf16[512,2048]{1,0:T(8,128)(2,1)S(1)}, bf16[512,2048]{1,0:T(8,128)(2,1)}, u32[]{:S(2)}) copy-start(bf16[512,2048]{1,0:T(8,128)(2,1)} %param.10) | copy-start | bytes 6291460
  67.2 105.8 %copy-start.17 = (bf16[128,6144]{0,1:T(8,128)(2,1)}, bf16[128,6144]{0,1:T(8,128)(2,1)S(1)}, u32[]{:S(2)}) copy-start(bf16[128,6144]{0,1:T(8,128)(2,1)S(1)} %add_convert_fusion) | copy-start | bytes 4718596
  180.0 20.4 %all-to-all-start = ((bf16[8,256,128]{2,1,0:T(8,128)(2,1)}), bf16[8,256,128]{2,1,0:T(8,128)(2,1)S(1)}, u32[]{:S(2)}, u32[]{:S(2)}) async-start(bf16[8,256,128]{2,1,0:T(8,128)(2,1)} %bitcast.14), calls=%async_computation | async-start | bytes 1048576 | tf_op jit(solution)/shard_map/all_to_all | solution.py:118
  200.5 18.9 %all-to-all-start.2 = ((bf16[8,256,128]{2,1,0:T(8,128)(2,1)}), bf16[8,256,128]{2,1,0:T(8,128)(2,1)S(1)}, u32[]{:S(2)}, u32[]{:S(2)}) async-start(bf16[8,256,128]{2,1,0:T(8,128)(2,1)} %bitcast.113), calls=%async_computation.2 | async-start | bytes 1048576 | tf_op jit(solution)/shard_map/all_to_all | solution.py:148
  219.4 75.9 %copy-start.11 = (bf16[8,256,128]{2,1,0:T(8,128)(2,1)}, bf16[8,256,128]{2,1,0:T(8,128)(2,1)S(1)}, u32[]{:S(2)}) copy-start(bf16[8,256,128]{2,1,0:T(8,128)(2,1)S(1)} %all-to-all-done.2) | copy-start | bytes 1572868
  258.4 6.2 %copy-start.13 = (f32[256,16,128]{0,2,1:T(8,128)S(1)}, f32[256,16,128]{0,2,1:T(8,128)}, u32[]{:S(2)}) copy-start(f32[256,16,128]{0,2,1:T(8,128)} %get-tuple-element.38) | copy-start | bytes 6291460
  258.4 6.2 %copy-start.14 = (f32[256,16,128]{0,2,1:T(8,128)S(1)}, f32[256,16,128]{0,2,1:T(8,128)}, u32[]{:S(2)}) copy-start(f32[256,16,128]{0,2,1:T(8,128)} %get-tuple-element.39) | copy-start | bytes 6291460
  272.4 6.2 %copy-start.15 = (f32[256,16,128]{0,2,1:T(8,128)S(1)}, f32[256,16,128]{0,2,1:T(8,128)}, u32[]{:S(2)}) copy-start(f32[256,16,128]{0,2,1:T(8,128)} %get-tuple-element.22) | copy-start | bytes 6291460
  272.4 6.2 %copy-start.16 = (f32[256,16,128]{0,2,1:T(8,128)S(1)}, f32[256,16,128]{0,2,1:T(8,128)}, u32[]{:S(2)}) copy-start(f32[256,16,128]{0,2,1:T(8,128)} %get-tuple-element.23) | copy-start | bytes 6291460
  299.4 19.5 %all-to-all-start.3 = ((bf16[256,8,128]{2,0,1:T(8,128)(2,1)}), bf16[256,8,128]{2,0,1:T(8,128)(2,1)}, u32[]{:S(2)}, u32[]{:S(2)}) async-start(bf16[256,8,128]{2,0,1:T(8,128)(2,1)} %copy.54), calls=%async_computation.3 | async-start | bytes 1048576 | tf_op jit(solution)/shard_map/all_to_all | solution.py:157
  303.6 220.1 %all-reduce.2.cloned.1.call-start = ((), (), s32[]{:S(2)}) async-start(), calls=%async_computation.6 | async-start | bytes 196608 | tf_op jit(solution)/shard_map/psum | solution.py:182
  303.6 34.2 %copy-start.18 = (bf16[128,6144]{0,1:T(8,128)(2,1)S(1)}, bf16[128,6144]{0,1:T(8,128)(2,1)}, u32[]{:S(2)}) copy-start(bf16[128,6144]{0,1:T(8,128)(2,1)} %copy-done.17) | copy-start | bytes 4718596
  318.9 21.0 %copy-start.22 = (f32[128,2048]{0,1:T(8,128)S(1)}, f32[128,2048]{0,1:T(8,128)}, u32[]{:S(2)}) copy-start(f32[128,2048]{0,1:T(8,128)} %get-tuple-element.57) | copy-start | bytes 3145732
  342.1 10.4 %slice-start = ((s8[6291456]{0:T(1024)(128)(4,1)}), s8[2097152]{0:T(1024)(128)(4,1)S(1)}, s32[]{:S(2)}) async-start(s8[6291456]{0:T(1024)(128)(4,1)} %bitcast.103), calls=%async_computation.9 | async-start | bytes 4194304
  344.0 3.1 collective-permute-start.4
  349.0 5.0 copy-start.7
  365.1 160.1 %reduce-scatter.3.cloned.1.call-start = ((), (), s32[]{:S(2)}) async-start(), calls=%async_computation.7 | async-start | bytes 1310720 | tf_op jit(solution)/shard_map/reduce_scatter | solution.py:162
  369.8 217.0 %reduce-scatter.5.cloned.1.call-start = ((), (), s32[]{:S(2)}) async-start(), calls=%async_computation.8 | async-start | bytes 17301504 | tf_op jit(solution)/shard_map/reduce_scatter | solution.py:138
  378.2 11.7 %copy-start.19 = (bf16[128,6144]{0,1:T(8,128)(2,1)S(1)}, bf16[128,6144]{0,1:T(8,128)(2,1)}, u32[]{:S(2)}) copy-start(bf16[128,6144]{0,1:T(8,128)(2,1)} %get-tuple-element.40) | copy-start | bytes 4718596
  (13 other events, 45.0 us)
Sparse Core Ops, SparseCore 0:
  365.2 158.3 all-reduce.1
Sparse Core Ops, SparseCore 1:
  369.9 26.3 reduce-scatter.2
  398.5 188.3 reduce-scatter.4
